TPU v7x, 32 devices: a whole 2x2x4 slice. The times are simulated.
32 devices in a mesh: tile: 4 (over y, core), dp: 8 (over z, x).
Axes of the slice: x: 2, y: 2, z: 4, core: 2. Of those that a mesh axis runs over, the one named last changes fastest.
Arguments:
- observed: float32 [8, 2, 8, 32], P('dp', None, 'tile'), may hold values from -6 to 6
- targets: float32 [8, 2, 8, 32], P('dp', None, 'tile'), may hold values from -6 to 6
- pixel_mask: int32 [8, 2, 8, 32], P('dp', None, 'tile'), may hold values 0 or 1
- lengths: int32 [8], P('dp'), may hold values from 1 to 2, as said below
- step_count: int32 [1], replicated, may hold values from 2 to 20
- kernels: float32 [1, 12800, 1024], P(None, 'dp'), may hold values from -0.0546875 to 0.0546875
- kernel_moment: float32 [1, 12800, 1024], P(None, 'dp'), may hold values from -7.6293945e-06 to 7.6293945e-06
- kernel_second: float32 [1, 12800, 1024], P(None, 'dp'), may hold values from 1.9073486e-12 to 7.6293945e-12
- norm_params: float32 [2, 1, 1024], replicated
- norm_moment: float32 [2, 1, 1024], replicated, may hold values from -1.5258789e-05 to 1.5258789e-05
- norm_second: float32 [2, 1, 1024], replicated, may hold values from 7.6293945e-12 to 3.0517578e-11
- end_params: float32 [3, 256], replicated
- end_moment: float32 [3, 256], replicated, may hold values from -7.6293945e-05 to 7.6293945e-05
- end_second: float32 [3, 256], replicated, may hold values from 1.9073486e-10 to 7.6293943e-10
- head_bias: float32 [1], replicated, may hold values from -3 to 3
- head_moment: float32 [1], replicated, may hold values from -0.0546875 to 0.0546875
- head_second: float32 [1], replicated, may hold values from 7.6293945e-05 to 0.00030517578
- hidden_init: float32 [1, 8, 8, 32, 256], P(None, 'dp', 'tile'), may hold values from -0.9 to 0.9
- cells_init: float32 [1, 8, 8, 32, 256], P(None, 'dp', 'tile'), may hold values from -5 to 5
Outputs:
- loss_value: float32 [], replicated
- grad_norm: float32 [], replicated
- kernels_new: float32 [1, 12800, 1024], P(None, 'dp')
- kernel_moment_new: float32 [1, 12800, 1024], P(None, 'dp')
- kernel_second_new: float32 [1, 12800, 1024], P(None, 'dp')
- norm_new: float32 [2, 1, 1024], replicated
- norm_moment_new: float32 [2, 1, 1024], replicated
- norm_second_new: float32 [2, 1, 1024], replicated
- end_new: float32 [3, 256], replicated
- end_moment_new: float32 [3, 256], replicated
- end_second_new: float32 [3, 256], replicated
- head_new: float32 [1], replicated
- head_moment_new: float32 [1], replicated
- head_second_new: float32 [1], replicated
- hidden_final: float32 [1, 8, 8, 32, 256], P(None, 'dp', 'tile')
- cells_final: float32 [1, 8, 8, 32, 256], P(None, 'dp', 'tile')
Inputs may be any that keep to these rules, and one draw needn't show every extreme that they name: `lengths`: some stream has all 2 frames counting and some only one.
All inputs are finite; a program needn't handle non-finite values. No bound on the sum of `pixel_mask` on one device may be relied on, other than what follows from the above.
Results may differ from a plain program's by a relative error of at most 0.0003.
The roundings to bfloat16 on the way count: a program that leaves them out, or rounds other values in their place, can miss the bound.
Values may be sent and summed in bfloat16 or wider, within the bound.
No kernel may reach another device: no remote copies, remote signals or barrier semaphores. Data moves between devices by JAX's collectives and lax.ppermute only.
A program may use at most 192 MiB of HBM per device.

v0:
```python
import jax
import jax.numpy as jnp
from jax import lax
from jax.sharding import PartitionSpec as P

IN_DIM = 512
KERNEL = 5
GROUP_SIZE = 64
clip_limit = 0.005
small_rate = 0.1


def padded_2(cells, sides, width):
    for axis, dim in sides:
        count = lax.axis_size(axis)
        ends = count - 1
        head = lax.slice_in_dim(cells, 0, width, axis=dim)
        tail = lax.slice_in_dim(cells, cells.shape[dim] - width, cells.shape[dim], axis=dim)
        cells = jnp.concatenate(
            [
                lax.ppermute(tail, axis, [(i, (i + 1) % count) for i in range(ends)]),
                cells,
                lax.ppermute(head, axis, [((i + 1) % count, i) for i in range(ends)]),
            ],
            axis=dim,
        )
    return cells


def group_norm(gates, gain, shift):
    full_shape = gates.shape
    grouped = gates.reshape(full_shape[:-1] + (full_shape[-1] // GROUP_SIZE, GROUP_SIZE))
    centred = grouped - jnp.mean(grouped, axis=-1, keepdims=True)
    spread = jnp.mean(centred * centred, axis=-1, keepdims=True)
    return (centred * lax.rsqrt(spread + 1e-05)).reshape(full_shape) * gain + shift


def lstm_cell(gates, cells_prev, gain, shift):
    normed = group_norm(gates, gain, shift)
    quarter = normed.shape[-1] // 4
    input_gate = jax.nn.sigmoid(normed[..., :quarter])
    forget_gate = jax.nn.sigmoid(normed[..., quarter : 2 * quarter])
    candidate = jnp.tanh(normed[..., 2 * quarter : 3 * quarter])
    output_gate = jax.nn.sigmoid(normed[..., 3 * quarter :])
    cells_next = forget_gate * cells_prev + input_gate * candidate
    return (output_gate * jnp.tanh(cells_next), cells_next)


def unfold(padded, rows, columns):
    pieces = []
    for row_off in range(KERNEL):
        for col_off in range(KERNEL):
            pieces.append(padded[:, row_off : row_off + rows, col_off : col_off + columns, :])
    joined = jnp.concatenate(pieces, axis=-1)
    return joined.reshape(-1, joined.shape[-1])


def pad_columns(values):
    margin = KERNEL // 2
    return jnp.pad(values, ((0, 0), (0, 0), (margin, margin), (0, 0)))


def layer_forward(weight_full, gain, shift, inputs_low, hidden_start, cells_start):
    rows, columns = (hidden_start.shape[1], hidden_start.shape[2])
    hidden_low = hidden_start.astype(jnp.bfloat16)
    cells = cells_start
    kept = []
    outputs = []
    outputs_low = []
    hidden = hidden_start
    for frame_no in range(len(inputs_low)):
        joined = jnp.concatenate([inputs_low[frame_no], hidden_low], axis=-1)
        padded = padded_2(joined, (("tile", 1),), KERNEL // 2)
        padded = pad_columns(padded)
        gates = jnp.dot(
            unfold(padded, rows, columns), weight_full, preferred_element_type=jnp.float32
        )
        gates = gates.reshape(hidden_start.shape[:3] + (weight_full.shape[1],))
        kept.append((padded, gates, cells))
        hidden, cells = lstm_cell(gates, cells, gain, shift)
        hidden_low = hidden.astype(jnp.bfloat16)
        outputs.append(hidden)
        outputs_low.append(hidden_low)
    return (outputs, outputs_low, kept, hidden, cells)


def layer_backward(weight_full, gain, shift, kept, grad_above):
    pixel_shape = kept[0][1].shape
    rows, columns, gate_dim = (pixel_shape[1], pixel_shape[2], pixel_shape[3])
    in_dim = weight_full.shape[0] // (KERNEL * KERNEL)
    half = in_dim // 2
    flipped = weight_full.reshape(KERNEL, KERNEL, in_dim, gate_dim)[::-1, ::-1]
    flipped = flipped.transpose(0, 1, 3, 2).reshape(KERNEL * KERNEL * gate_dim, in_dim)
    grad_weight = jnp.zeros(weight_full.shape, jnp.float32)
    grad_gain = jnp.zeros(gain.shape, jnp.float32)
    grad_shift = jnp.zeros(shift.shape, jnp.float32)
    grad_hidden = jnp.zeros(pixel_shape[:3] + (half,), jnp.float32)
    grad_cells = jnp.zeros(pixel_shape[:3] + (half,), jnp.float32)
    grad_inputs = [None] * len(kept)
    for frame_no in reversed(range(len(kept))):
        padded, gates, cells_prev = kept[frame_no]
        unused, pull = jax.vjp(lstm_cell, gates, cells_prev, gain, shift)
        grad_gates, grad_cells, part_gain, part_shift = pull(
            (grad_above[frame_no] + grad_hidden, grad_cells)
        )
        grad_gain = grad_gain + part_gain
        grad_shift = grad_shift + part_shift
        gates_low = grad_gates.astype(jnp.bfloat16)
        grad_weight = grad_weight + lax.dot_general(
            unfold(padded, rows, columns),
            gates_low.reshape(-1, gate_dim),
            (((0,), (0,)), ((), ())),
            preferred_element_type=jnp.float32,
        )
        spread = padded_2(gates_low, (("tile", 1),), KERNEL // 2)
        spread = pad_columns(spread)
        grad_joined = jnp.dot(
            unfold(spread, rows, columns), flipped, preferred_element_type=jnp.float32
        )
        grad_joined = grad_joined.reshape(pixel_shape[:3] + (in_dim,))
        grad_inputs[frame_no] = grad_joined[..., :half]
        grad_hidden = grad_joined[..., half:]
    return (grad_weight, grad_gain, grad_shift, grad_inputs)


def adamw(weight, moment, second, grad, rate, correction):
    moment_new = 0.5 * moment + 0.5 * grad
    second_new = 0.5 * second + 0.5 * grad * grad
    update = moment_new / correction / (jnp.sqrt(second_new / correction) + 1e-08)
    return (weight - rate * (update + 0.01 * weight), moment_new, second_new)


def per_device(
    observed,
    targets,
    pixel_mask,
    lengths,
    step_count,
    kernels,
    kernel_moment,
    kernel_second,
    norm_params,
    norm_moment,
    norm_second,
    end_params,
    end_moment,
    end_second,
    head_bias,
    head_moment,
    head_second,
    hidden_init,
    cells_init,
):
    frame_total = observed.shape[1]
    layers = kernels.shape[0]
    frame_ids = lax.broadcasted_iota(jnp.int32, (1, frame_total), 1)
    counted = (frame_ids < lengths[:, None]).astype(jnp.float32)
    valid = pixel_mask.astype(jnp.float32) * counted[:, :, None, None]
    count = jnp.maximum(lax.psum(jnp.sum(valid), ("tile", "dp")), 1.0)
    inputs_low = [
        (end_params[0] * observed[:, frame_no, :, :, None] + end_params[1]).astype(jnp.bfloat16)
        for frame_no in range(frame_total)
    ]
    outputs = []
    layer_no = 0
    weight_full = lax.all_gather(kernels[layer_no].astype(jnp.bfloat16), "dp", axis=0, tiled=True)
    outputs, outputs_low, kept, hidden, cells = layer_forward(
        weight_full,
        norm_params[0, layer_no],
        norm_params[1, layer_no],
        inputs_low,
        hidden_init[layer_no],
        cells_init[layer_no],
    )
    stored_kept = [kept]
    hidden_list = [hidden]
    cells_list = [cells]
    loss_sum = jnp.zeros((), jnp.float32)
    grad_head_weight = jnp.zeros(end_params.shape[1:], jnp.float32)
    grad_head = jnp.zeros((1,), jnp.float32)
    grad_above = []
    for frame_no in range(frame_total):
        predicted = jnp.sum(outputs[frame_no] * end_params[2], axis=-1) + head_bias[0]
        error = predicted - targets[:, frame_no]
        weighted = valid[:, frame_no] * error
        loss_sum = loss_sum + jnp.sum(weighted * error)
        grad_pred = 2.0 * weighted / count
        grad_head = grad_head + jnp.sum(grad_pred)
        grad_head_weight = grad_head_weight + jnp.sum(
            grad_pred[..., None] * outputs[frame_no], axis=(0, 1, 2)
        )
        grad_above.append(grad_pred[..., None] * end_params[2])
    kernel_grads = [None] * layers
    gain_grads = [None] * layers
    shift_grads = [None] * layers
    for layer_no in reversed(range(layers)):
        weight_full = lax.all_gather(
            kernels[layer_no].astype(jnp.bfloat16), "dp", axis=0, tiled=True
        )
        grad_weight, grad_gain, grad_shift, grad_inputs = layer_backward(
            weight_full,
            norm_params[0, layer_no],
            norm_params[1, layer_no],
            stored_kept[layer_no],
            grad_above,
        )
        kernel_grads[layer_no] = grad_weight
        gain_grads[layer_no] = grad_gain
        shift_grads[layer_no] = grad_shift
        grad_above = grad_inputs
    grad_lift_weight = jnp.zeros(end_params.shape[1:], jnp.float32)
    grad_lift_bias = jnp.zeros(end_params.shape[1:], jnp.float32)
    for frame_no in range(frame_total):
        grad_lift_weight = grad_lift_weight + jnp.sum(
            grad_above[frame_no] * observed[:, frame_no, :, :, None], axis=(0, 1, 2)
        )
        grad_lift_bias = grad_lift_bias + jnp.sum(grad_above[frame_no], axis=(0, 1, 2))
    grad_norms = jnp.stack([jnp.stack(gain_grads), jnp.stack(shift_grads)])
    grad_ends = jnp.stack([grad_lift_weight, grad_lift_bias, grad_head_weight])
    grad_kernels = jnp.stack(kernel_grads)
    shard = lax.psum_scatter(grad_kernels, "dp", scatter_dimension=1, tiled=True)
    shard = lax.psum(shard, "tile")
    local_square = jnp.sum(shard * shard)
    grad_norms, grad_ends, grad_head, loss_sum = lax.psum(
        (grad_norms, grad_ends, grad_head, loss_sum), ("tile", "dp")
    )
    kernel_square = lax.psum(local_square, "dp")
    squares = (
        kernel_square
        + jnp.sum(grad_norms * grad_norms)
        + jnp.sum(grad_ends * grad_ends)
        + jnp.sum(grad_head * grad_head)
    )
    grad_norm = jnp.sqrt(squares)
    factor = clip_limit / jnp.maximum(grad_norm, clip_limit)
    correction = 1.0 - jnp.power(0.5, step_count[0].astype(jnp.float32))
    kernel_rate = (KERNEL * KERNEL * IN_DIM) ** (-0.5)
    kern_out = adamw(kernels, kernel_moment, kernel_second, shard * factor, kernel_rate, correction)
    norm_out = adamw(
        norm_params, norm_moment, norm_second, grad_norms * factor, small_rate, correction
    )
    end_out = adamw(end_params, end_moment, end_second, grad_ends * factor, small_rate, correction)
    head_out = adamw(
        head_bias, head_moment, head_second, grad_head * factor, small_rate, correction
    )
    loss_value = loss_sum / count
    return (
        loss_value,
        grad_norm,
        kern_out[0],
        kern_out[1],
        kern_out[2],
        norm_out[0],
        norm_out[1],
        norm_out[2],
        end_out[0],
        end_out[1],
        end_out[2],
        head_out[0],
        head_out[1],
        head_out[2],
        jnp.stack(hidden_list),
        jnp.stack(cells_list),
    )


def solution(mesh):
    placed = (
        P("dp", None, "tile", None),
        P("dp", None, "tile", None),
        P("dp", None, "tile", None),
        P("dp"),
        P(),
        P(None, "dp", None),
        P(None, "dp", None),
        P(None, "dp", None),
        P(),
        P(),
        P(),
        P(),
        P(),
        P(),
        P(),
        P(),
        P(),
        P(None, "dp", "tile", None, None),
        P(None, "dp", "tile", None, None),
    )
    return jax.shard_map(
        per_device,
        mesh=mesh,
        in_specs=placed,
        out_specs=(
            P(),
            P(),
            P(None, "dp", None),
            P(None, "dp", None),
            P(None, "dp", None),
            P(),
            P(),
            P(),
            P(),
            P(),
            P(),
            P(),
            P(),
            P(),
            P(None, "dp", "tile", None, None),
            P(None, "dp", "tile", None, None),
        ),
        check_vma=False,
    )
```

profile of v0, /device:TPU:0, one launch (start us, length us, event | category | flops | bytes accessed | tf_op | source)
XLA Modules:
  0.0 1688.5 jit_solution(5633768059832277343)
XLA Ops:
  7.2 5.1 convert_element_type.95
  13.2 1.3 collective-permute-start.1
  14.5 3.0 collective-permute-start
  18.9 85.6 %psum.50 = f32[]{:T(128)} all-reduce(f32[]{:T(128)} %get-tuple-element.65), channel_id=1, replica_groups=mesh['tile'=4,'dp'=8] {'tile','dp'}, use_global_device_ids=true, to_apply=%region_10.11 | all-reduce | flops 1 | bytes 8 | tf_op jit(solution)/shard_map/psum | solution.py:159
  108.5 408.1 %all-gather.3.cloned.1.call-done = bf16[1,12800,1024]{2,1,0:T(8,128)(2,1)} async-done(((bf16[1,1600,1024]{2,1,0:T(8,128)(2,1)}), bf16[1,12800,1024]{2,1,0:T(8,128)(2,1)}) %all-gather.3.cloned.1.call-update) | async-done | bytes 26214416 | tf_op jit(solution)/shard_map/all_gather | solution.py:166
  516.7 10.8 fusion.3
  530.1 1.3 collective-permute-start.3
  531.4 3.0 collective-permute-start.2
  534.4 18.4 %reverse_bitcast_fusion = bf16[5,5,1024,512]{2,3,1,0:T(8,128)(2,1)} fusion(bf16[5,5,512,1024]{3,2,1,0:T(8,128)(2,1)} %bitcast.214), kind=kLoop, calls=%fused_computation.6 | loop fusion | bytes 52428800 | tf_op jit(solution)/shard_map/transpose | solution.py:93
  552.8 33.9 %copy.35 = bf16[5,5,1024,512]{3,2,1,0:T(8,128)(2,1)} copy(bf16[5,5,1024,512]{2,3,1,0:T(8,128)(2,1)} %reverse_bitcast_fusion) | data formatting | bytes 52428800 | tf_op jit(solution)/shard_map/transpose | solution.py:93
  588.8 10.8 fusion.1
  606.1 1.3 collective-permute-start.5
  607.4 3.8 collective-permute-start.4
  611.2 21.6 %fusion.11 = f32[12800,1024,1]{1,0,2:T(8,128)} fusion(bf16[1,2,32,12800]{3,2,1,0:T(8,128)(2,1)} %copy-done, bf16[1,2,32,1024]{3,2,1,0:T(8,128)(2,1)S(1)} %fusion.25), kind=kOutput, calls=%fused_computation.17 | convolution fusion | flops 1677721600 | bytes 54198272 | tf_op jit(solution)/shard_map/dot_general | solution.py:109
  633.8 10.8 fusion.13
  647.9 33.5 %fusion = f32[1,12800,1024]{2,1,0:T(8,128)} fusion(f32[12800,1024,1]{1,0,2:T(8,128)} %fusion.11, bf16[1,2,32,12800]{3,2,1,0:T(8,128)(2,1)S(1)} %copy-done.2, bf16[1,2,32,1024]{3,2,1,0:T(8,128)(2,1)S(1)} %fusion.27), kind=kOutput, calls=%fused_computation.1 | convolution fusion | flops 1690828800 | bytes 106627072 | tf_op jit(solution)/shard_map/dot_general | solution.py:109
  684.8 4.5 collective-permute-start.6
  705.7 793.9 %reduce-scatter.2.cloned.1.call-done = f32[1,1600,1024]{2,1,0:T(8,128)} async-done(((f32[1,12800,1024]{2,1,0:T(8,128)}), f32[1,1600,1024]{2,1,0:T(8,128)}) %reduce-scatter.2.cloned.1.call-update) | async-done | bytes 6553616 | tf_op jit(solution)/shard_map/reduce_scatter | solution.py:221
  1503.7 12.9 fusion.16
  1516.8 41.4 %all-reduce.12 = (f32[]{:T(128)}, f32[2,1,1024]{2,1,0:T(1,128)S(1)}, f32[3,256]{1,0:T(4,128)S(1)}, f32[1]{0:T(128)}) all-reduce(f32[]{:T(128)S(6)} %add.410, f32[2,1,1024]{2,1,0:T(1,128)S(1)} %pad_maximum_fusion.14, f32[3,256]{1,0:T(4,128)S(1)} %pad_maximum_fusion.15, f32[1]{0:T(128)} %bitcast.95), channel_id=1, replica_groups=mesh['tile'=4,'dp'=8] {'tile','dp'}, use_global_device_ids=true, to_apply=%region_8.9 | all-reduce | flops 2818 | bytes 22544 | tf_op jit(solution)/shard_map/psum | solution.py:224
  1560.1 66.4 %all-reduce.15.cloned.1.call-done = f32[1,1600,1024]{2,1,0:T(8,128)} async-done(((f32[1,1600,1024]{2,1,0:T(8,128)}), f32[1,1600,1024]{2,1,0:T(8,128)}) %all-reduce.15.cloned.1.call-update) | async-done | bytes 6553616 | tf_op jit(solution)/shard_map/psum | solution.py:222
  1626.4 5.1 multiply_reduce_fusion
  1632.9 22.0 %psum.52 = f32[]{:T(128)} all-reduce(f32[]{:T(128)} %multiply_reduce_fusion), channel_id=1, replica_groups=mesh['tile'=4,'dp'=8] {'dp'}, use_global_device_ids=true, to_apply=%region_18.19 | all-reduce | flops 1 | bytes 8 | tf_op jit(solution)/shard_map/psum | solution.py:227
  1659.0 17.3 %multiply_subtract_fusion = (f32[1,1600,1024]{2,1,0:T(8,128)}, f32[1,1600,1024]{2,1,0:T(8,128)}, f32[1,1600,1024]{2,1,0:T(8,128)}) fusion(f32[1,1600,1024]{2,1,0:T(8,128)} %param.24, f32[]{:T(128)} %bitcast.97, f32[1,1600,1024]{2,1,0:T(8,128)} %all-reduce.15.cloned.1.call-done, f32[]{:T(128)} %div.177, f32[1,1600,1024]{2,1,0:T(8,128)} %param.26, ...), kind=kLoop, calls=%fused_computation.10 | loop fusion | flops 24576000 | bytes 45875208 | tf_op jit(solution)/shard_map/sub | solution.py:130
  (289 shorter events, 40.2 us)
Async XLA Ops:
  7.2 509.5 %all-gather.3.cloned.1.call-start = ((), (), s32[]{:S(2)}) async-start(), calls=%async_computation.3 | async-start | bytes 29491200 | tf_op jit(solution)/shard_map/all_gather | solution.py:166
  12.3 5.9 copy-start.7
  12.3 5.9 copy-start.19
  12.4 1487.3 %reduce-scatter.2.cloned.1.call-start = ((), (), s32[]{:S(2)}) async-start(), calls=%async_computation.1 | async-start | bytes 58982400 | tf_op jit(solution)/shard_map/reduce_scatter | solution.py:221
  13.0 93.6 %copy-start.9 = (f32[2,32]{1,0:T(2,128)}, f32[2,32]{1,0:T(2,128)S(1)}, u32[]{:S(2)}) copy-start(f32[2,32]{1,0:T(2,128)S(1)} %get-tuple-element.135) | copy-start | bytes 772
  13.2 92.8 %collective-permute-start.1 = (bf16[1,2,32,512]{3,2,1,0:T(8,128)(2,1)S(1)}, bf16[1,2,32,512]{3,2,1,0:T(8,128)(2,1)S(1)}, u32[]{:S(2)}, u32[]{:S(2)}) collective-permute-start(bf16[1,2,32,512]{3,2,1,0:T(8,128)(2,1)S(1)} %pad_maximum_fusion.12), channel_id=1, source_target_pairs={{8,0},{16,8},{24,16},{9,1},{17,9},{25,17},{10,2},{18,10},{26,18},{... | collective-permute-start | bytes 196616 | tf_op jit(solution)/shard_map/ppermute | solution.py:23
  14.5 91.5 %collective-permute-start = (bf16[1,2,32,512]{3,2,1,0:T(8,128)(2,1)S(1)}, bf16[1,2,32,512]{3,2,1,0:T(8,128)(2,1)S(1)}, u32[]{:S(2)}, u32[]{:S(2)}) collective-permute-start(bf16[1,2,32,512]{3,2,1,0:T(8,128)(2,1)S(1)} %pad_maximum_fusion.12), channel_id=1, source_target_pairs={{0,8},{8,16},{16,24},{1,9},{9,17},{17,25},{2,10},{10,18},{18,26},{... | collective-permute-start | bytes 196616 | tf_op jit(solution)/shard_map/ppermute | solution.py:21
  530.1 56.6 %collective-permute-start.3 = (bf16[1,2,32,512]{3,2,1,0:T(8,128)(2,1)S(1)}, bf16[1,2,32,512]{3,2,1,0:T(8,128)(2,1)S(1)}, u32[]{:S(2)}, u32[]{:S(2)}) collective-permute-start(bf16[1,2,32,512]{3,2,1,0:T(8,128)(2,1)S(1)} %pad_maximum_fusion.13), channel_id=1, source_target_pairs={{8,0},{16,8},{24,16},{9,1},{17,9},{25,17},{10,2},{18,10},{26,18},{... | collective-permute-start | bytes 196616 | tf_op jit(solution)/shard_map/ppermute | solution.py:23
  531.4 55.3 %collective-permute-start.2 = (bf16[1,2,32,512]{3,2,1,0:T(8,128)(2,1)S(1)}, bf16[1,2,32,512]{3,2,1,0:T(8,128)(2,1)S(1)}, u32[]{:S(2)}, u32[]{:S(2)}) collective-permute-start(bf16[1,2,32,512]{3,2,1,0:T(8,128)(2,1)S(1)} %pad_maximum_fusion.13), channel_id=1, source_target_pairs={{0,8},{8,16},{16,24},{1,9},{9,17},{17,25},{2,10},{10,18},{18,26},{... | collective-permute-start | bytes 196616 | tf_op jit(solution)/shard_map/ppermute | solution.py:21
  601.1 1.8 copy-start.15
  602.8 41.9 %copy-start.3 = (f32[1,2,32,256]{3,2,1,0:T(8,128)}, f32[1,2,32,256]{3,2,1,0:T(8,128)S(1)}, u32[]{:S(2)}) copy-start(f32[1,2,32,256]{3,2,1,0:T(8,128)S(1)} %get-tuple-element.37) | copy-start | bytes 196612
  606.1 26.7 %collective-permute-start.5 = (bf16[1,2,32,1024]{3,2,1,0:T(8,128)(2,1)S(1)}, bf16[1,2,32,1024]{3,2,1,0:T(8,128)(2,1)S(1)}, u32[]{:S(2)}, u32[]{:S(2)}) collective-permute-start(bf16[1,2,32,1024]{3,2,1,0:T(8,128)(2,1)S(1)} %fusion.25), channel_id=1, source_target_pairs={{8,0},{16,8},{24,16},{9,1},{17,9},{25,17},{10,2},{18,10},{26,18},{... | collective-permute-start | bytes 393224 | tf_op jit(solution)/shard_map/ppermute | solution.py:23
  607.4 25.4 %collective-permute-start.4 = (bf16[1,2,32,1024]{3,2,1,0:T(8,128)(2,1)S(1)}, bf16[1,2,32,1024]{3,2,1,0:T(8,128)(2,1)S(1)}, u32[]{:S(2)}, u32[]{:S(2)}) collective-permute-start(bf16[1,2,32,1024]{3,2,1,0:T(8,128)(2,1)S(1)} %fusion.25), channel_id=1, source_target_pairs={{0,8},{8,16},{16,24},{1,9},{9,17},{17,25},{2,10},{10,18},{18,26},{... | collective-permute-start | bytes 393224 | tf_op jit(solution)/shard_map/ppermute | solution.py:21
  633.8 11.0 copy-start.6
  681.5 944.9 %all-reduce.15.cloned.1.call-start = ((), (), s32[]{:S(2)}) async-start(), calls=%async_computation.2 | async-start | bytes 13107200 | tf_op jit(solution)/shard_map/psum | solution.py:222
  683.5 9.1 collective-permute-start.7
  684.8 7.8 collective-permute-start.6
  1503.7 12.9 copy-start.10
  1560.0 97.7 %copy-start.8 = (f32[2,1,1024]{2,1,0:T(1,128)S(1)}, f32[2,1,1024]{2,1,0:T(1,128)}, u32[]{:S(2)}) copy-start(f32[2,1,1024]{2,1,0:T(1,128)} %param.27) | copy-start | bytes 24580
  1560.0 97.7 %copy-start.13 = (f32[2,1,1024]{2,1,0:T(1,128)S(1)}, f32[2,1,1024]{2,1,0:T(1,128)}, u32[]{:S(2)}) copy-start(f32[2,1,1024]{2,1,0:T(1,128)} %param.29) | copy-start | bytes 24580
  1560.0 97.7 %copy-start.14 = (f32[2,1,1024]{2,1,0:T(1,128)S(1)}, f32[2,1,1024]{2,1,0:T(1,128)}, u32[]{:S(2)}) copy-start(f32[2,1,1024]{2,1,0:T(1,128)} %param.28) | copy-start | bytes 24580
  1560.0 98.3 %copy-start.12 = (f32[3,256]{1,0:T(4,128)S(1)}, f32[3,256]{1,0:T(4,128)}, u32[]{:S(2)}) copy-start(f32[3,256]{1,0:T(4,128)} %param.30) | copy-start | bytes 9220
  1560.0 98.3 %copy-start.16 = (f32[3,256]{1,0:T(4,128)S(1)}, f32[3,256]{1,0:T(4,128)}, u32[]{:S(2)}) copy-start(f32[3,256]{1,0:T(4,128)} %param.32) | copy-start | bytes 9220
  1560.0 98.3 %copy-start.17 = (f32[3,256]{1,0:T(4,128)S(1)}, f32[3,256]{1,0:T(4,128)}, u32[]{:S(2)}) copy-start(f32[3,256]{1,0:T(4,128)} %param.31) | copy-start | bytes 9220
  (7 other events, 7.4 us)
Sparse Core Ops, SparseCore 0:
  12.5 504.1 all-gather.2
  681.6 817.9 reduce-scatter.1
  1502.0 124.3 all-reduce.14
where the time goes:
time: 1690 us
  waiting for transfers between devices  1270 us (75%)
  blocking collectives  149 us (9%)
  matrix products  100 us (6%)
  local copies, waits for them, and re-layouts  76.5 us (5%)
  other arithmetic  41.9 us (2%)
  between operations  32.4 us (2%)
  starting transfers between devices  19.7 us (1%)
    reduce_scatter x1, waiting for transfers between devices, per_device(): lax.psum_scatter(grad_kernels, 'dp', scatter_dimension=1, tiled=True)  794 us
    all_gather x1, waiting for transfers between devices, per_device(): lax.all_gather(kernels[layer_no].astype(jnp.bfloat16), 'dp', axis=0, tile...  408 us
    psum x1, blocking collectives, per_device(): count = jnp.maximum(lax.psum(jnp.sum(valid), ('tile', 'dp')), 1.0)  85.6 us
    psum x1, waiting for transfers between devices, per_device(): shard = lax.psum(shard, 'tile')  66.4 us
    dot_general x2, matrix products, layer_backward(): lax.dot_general(unfold(padded, rows, columns), gates_low.reshape(-1, gate...  55.1 us
    transpose x2, local copies, waits for them, and re-layouts, layer_backward(): flipped.transpose(0, 1, 3, 2).reshape(KERNEL * KERNEL * gate_dim, in_dim)  52.3 us
    psum x1, blocking collectives, per_device(): lax.psum((grad_norms, grad_ends, grad_head, loss_sum), ('tile', 'dp'))  41.4 us
  transfers between devices with their start and end apart: 11, of which 3 were waited for; matrix products, arithmetic and copies ran while one was open for 6% of the time, Pallas kernels for 0%

commit v1 on v0

--- a/solution.py
+++ b/solution.py
@@ -219,7 +219,7 @@
     grad_ends = jnp.stack([grad_lift_weight, grad_lift_bias, grad_head_weight])
     grad_kernels = jnp.stack(kernel_grads)
     shard = lax.psum_scatter(grad_kernels, "dp", scatter_dimension=1, tiled=True)
-    shard = lax.psum(shard, "tile")
+    shard = lax.all_gather(shard, axis_name="tile").sum(axis=0)
     local_square = jnp.sum(shard * shard)
     grad_norms, grad_ends, grad_head, loss_sum = lax.psum(
         (grad_norms, grad_ends, grad_head, loss_sum), ("tile", "dp")

time: 1690 us -> 1740 us (1.030)
  waiting for transfers between devices: 1270 us -> 1320 us
    all_gather x0 -> x1, waiting for transfers between devices: none -> 91 us  [per_device(): shard = lax.all_gather(shard, axis_name='tile').sum(axis=0)]
    psum x1 -> x0, waiting for transfers between devices: 66.4 us -> none  [per_device(): shard = lax.psum(shard, 'tile')]
    reduce_scatter x1, waiting for transfers between devices: 794 us -> 818 us  [per_device(): lax.psum_scatter(grad_kernels, 'dp', scatter_dimension=1, tiled=True)]
  transfers between devices with their start and end apart: 11 -> 11, of which waited for: 3 -> 3; matrix products, arithmetic and copies ran while one was open for 6% -> 5% of each run, Pallas kernels for 0% -> 0%
where the time goes in v1:
time: 1740 us
  waiting for transfers between devices  1320 us (76%)
  blocking collectives  150 us (9%)
  matrix products  104 us (6%)
  local copies, waits for them, and re-layouts  61.5 us (4%)
  other arithmetic  56.1 us (3%)
  between operations  32.6 us (2%)
  starting transfers between devices  18.4 us (1%)
    reduce_scatter x1, waiting for transfers between devices, per_device(): lax.psum_scatter(grad_kernels, 'dp', scatter_dimension=1, tiled=True)  818 us
    all_gather x1, waiting for transfers between devices, per_device(): lax.all_gather(kernels[layer_no].astype(jnp.bfloat16), 'dp', axis=0, tile...  408 us
    all_gather x1, waiting for transfers between devices, per_device(): shard = lax.all_gather(shard, axis_name='tile').sum(axis=0)  91 us
    psum x1, blocking collectives, per_device(): count = jnp.maximum(lax.psum(jnp.sum(valid), ('tile', 'dp')), 1.0)  85.6 us
    dot_general x2, matrix products, layer_backward(): lax.dot_general(unfold(padded, rows, columns), gates_low.reshape(-1, gate...  55.1 us
    transpose x2, local copies, waits for them, and re-layouts, layer_backward(): flipped.transpose(0, 1, 3, 2).reshape(KERNEL * KERNEL * gate_dim, in_dim)  52.3 us
    psum x1, blocking collectives, per_device(): lax.psum((grad_norms, grad_ends, grad_head, loss_sum), ('tile', 'dp'))  41.9 us
  transfers between devices with their start and end apart: 11, of which 3 were waited for; matrix products, arithmetic and copies ran while one was open for 5% of the time, Pallas kernels for 0%

profile of v1, /device:TPU:0, one launch (start us, length us, event | category | flops | bytes accessed | tf_op | source)
XLA Modules:
  0.0 1739.9 jit_solution(17214514871701624718)
XLA Ops:
  7.2 5.1 convert_element_type.95
  13.2 1.3 collective-permute-start.1
  14.5 3.0 collective-permute-start
  18.9 85.6 %psum.43 = f32[]{:T(128)} all-reduce(f32[]{:T(128)} %get-tuple-element.65), channel_id=1, replica_groups=mesh['tile'=4,'dp'=8] {'tile','dp'}, use_global_device_ids=true, to_apply=%region_10.11 | all-reduce | flops 1 | bytes 8 | tf_op jit(solution)/shard_map/psum | solution.py:159
  108.5 408.1 %all-gather.5.cloned.1.call-done = bf16[1,12800,1024]{2,1,0:T(8,128)(2,1)} async-done(((bf16[1,1600,1024]{2,1,0:T(8,128)(2,1)}), bf16[1,12800,1024]{2,1,0:T(8,128)(2,1)}) %all-gather.5.cloned.1.call-update) | async-done | bytes 26214416 | tf_op jit(solution)/shard_map/all_gather | solution.py:166
  516.7 10.8 fusion.3
  530.1 1.3 collective-permute-start.3
  531.4 3.0 collective-permute-start.2
  534.4 18.4 %reverse_bitcast_fusion = bf16[5,5,1024,512]{2,3,1,0:T(8,128)(2,1)} fusion(bf16[5,5,512,1024]{3,2,1,0:T(8,128)(2,1)} %bitcast.219), kind=kLoop, calls=%fused_computation.6 | loop fusion | bytes 52428800 | tf_op jit(solution)/shard_map/transpose | solution.py:93
  552.8 33.9 %copy.36 = bf16[5,5,1024,512]{3,2,1,0:T(8,128)(2,1)} copy(bf16[5,5,1024,512]{2,3,1,0:T(8,128)(2,1)} %reverse_bitcast_fusion) | data formatting | bytes 52428800 | tf_op jit(solution)/shard_map/transpose | solution.py:93
  588.8 10.8 fusion.1
  607.9 3.8 collective-permute-start.4
  611.7 21.6 %fusion.11 = f32[12800,1024,1]{1,0,2:T(8,128)} fusion(bf16[1,2,32,12800]{3,2,1,0:T(8,128)(2,1)} %copy-done, bf16[1,2,32,1024]{3,2,1,0:T(8,128)(2,1)S(1)} %fusion.25), kind=kOutput, calls=%fused_computation.17 | convolution fusion | flops 1677721600 | bytes 54198272 | tf_op jit(solution)/shard_map/dot_general | solution.py:109
  634.4 10.8 fusion.13
  649.1 33.5 %fusion = f32[1,12800,1024]{2,1,0:T(8,128)} fusion(f32[12800,1024,1]{1,0,2:T(8,128)} %fusion.11, bf16[1,2,32,12800]{3,2,1,0:T(8,128)(2,1)S(1)} %copy-done.2, bf16[1,2,32,1024]{3,2,1,0:T(8,128)(2,1)S(1)} %fusion.27), kind=kOutput, calls=%fused_computation.1 | convolution fusion | flops 1690828800 | bytes 106627072 | tf_op jit(solution)/shard_map/dot_general | solution.py:109
  682.7 818.0 %reduce-scatter.2.cloned.1.call-done = f32[1,1600,1024]{2,1,0:T(8,128)} async-done(((f32[1,12800,1024]{2,1,0:T(8,128)}), f32[1,1600,1024]{2,1,0:T(8,128)}) %reduce-scatter.2.cloned.1.call-update) | async-done | bytes 6553616 | tf_op jit(solution)/shard_map/reduce_scatter | solution.py:221
  1504.0 3.3 collective-permute-start.6
  1511.6 16.9 fusion.16
  1528.7 41.9 %all-reduce.12 = (f32[]{:T(128)}, f32[2,1,1024]{2,1,0:T(1,128)S(1)}, f32[3,256]{1,0:T(4,128)S(1)}, f32[1]{0:T(128)}) all-reduce(f32[]{:T(128)S(6)} %add.408, f32[2,1,1024]{2,1,0:T(1,128)S(1)} %pad_maximum_fusion.14, f32[3,256]{1,0:T(4,128)S(1)} %pad_maximum_fusion.15, f32[1]{0:T(128)} %bitcast.95), channel_id=1, replica_groups=mesh['tile'=4,'dp'=8] {'tile','dp'}, use_global_device_ids=true, to_apply=%region_8.9 | all-reduce | flops 2818 | bytes 22544 | tf_op jit(solution)/shard_map/psum | solution.py:224
  1572.5 91.0 %all-gather.7.cloned.1.call-done = f32[4,1600,1024]{2,1,0:T(8,128)} async-done(((f32[1,1600,1024]{2,1,0:T(8,128)}), f32[4,1600,1024]{2,1,0:T(8,128)}) %all-gather.7.cloned.1.call-update) | async-done | bytes 26214416 | tf_op jit(solution)/shard_map/all_gather | solution.py:222
  1663.4 14.3 reduce.16
  1677.7 5.1 multiply_reduce_fusion
  1684.2 22.0 %psum.44 = f32[]{:T(128)} all-reduce(f32[]{:T(128)} %multiply_reduce_fusion), channel_id=1, replica_groups=mesh['tile'=4,'dp'=8] {'dp'}, use_global_device_ids=true, to_apply=%region_18.19 | all-reduce | flops 1 | bytes 8 | tf_op jit(solution)/shard_map/psum | solution.py:227
  1709.1 17.3 multiply_subtract_fusion
  (296 shorter events, 26.3 us)
Async XLA Ops:
  7.2 509.5 %all-gather.5.cloned.1.call-start = ((), (), s32[]{:S(2)}) async-start(), calls=%async_computation.2 | async-start | bytes 29491200 | tf_op jit(solution)/shard_map/all_gather | solution.py:166
  12.4 1488.3 %reduce-scatter.2.cloned.1.call-start = ((), (), s32[]{:S(2)}) async-start(), calls=%async_computation.1 | async-start | bytes 58982400 | tf_op jit(solution)/shard_map/reduce_scatter | solution.py:221
  13.0 93.6 %copy-start.9 = (f32[2,32]{1,0:T(2,128)}, f32[2,32]{1,0:T(2,128)S(1)}, u32[]{:S(2)}) copy-start(f32[2,32]{1,0:T(2,128)S(1)} %get-tuple-element.135) | copy-start | bytes 772
  13.2 92.8 %collective-permute-start.1 = (bf16[1,2,32,512]{3,2,1,0:T(8,128)(2,1)S(1)}, bf16[1,2,32,512]{3,2,1,0:T(8,128)(2,1)S(1)}, u32[]{:S(2)}, u32[]{:S(2)}) collective-permute-start(bf16[1,2,32,512]{3,2,1,0:T(8,128)(2,1)S(1)} %pad_maximum_fusion.12), channel_id=1, source_target_pairs={{8,0},{16,8},{24,16},{9,1},{17,9},{25,17},{10,2},{18,10},{26,18},{... | collective-permute-start | bytes 196616 | tf_op jit(solution)/shard_map/ppermute | solution.py:23
  14.5 91.5 %collective-permute-start = (bf16[1,2,32,512]{3,2,1,0:T(8,128)(2,1)S(1)}, bf16[1,2,32,512]{3,2,1,0:T(8,128)(2,1)S(1)}, u32[]{:S(2)}, u32[]{:S(2)}) collective-permute-start(bf16[1,2,32,512]{3,2,1,0:T(8,128)(2,1)S(1)} %pad_maximum_fusion.12), channel_id=1, source_target_pairs={{0,8},{8,16},{16,24},{1,9},{9,17},{17,25},{2,10},{10,18},{18,26},{... | collective-permute-start | bytes 196616 | tf_op jit(solution)/shard_map/ppermute | solution.py:21
  530.1 56.6 %collective-permute-start.3 = (bf16[1,2,32,512]{3,2,1,0:T(8,128)(2,1)S(1)}, bf16[1,2,32,512]{3,2,1,0:T(8,128)(2,1)S(1)}, u32[]{:S(2)}, u32[]{:S(2)}) collective-permute-start(bf16[1,2,32,512]{3,2,1,0:T(8,128)(2,1)S(1)} %pad_maximum_fusion.13), channel_id=1, source_target_pairs={{8,0},{16,8},{24,16},{9,1},{17,9},{25,17},{10,2},{18,10},{26,18},{... | collective-permute-start | bytes 196616 | tf_op jit(solution)/shard_map/ppermute | solution.py:23
  531.4 55.3 %collective-permute-start.2 = (bf16[1,2,32,512]{3,2,1,0:T(8,128)(2,1)S(1)}, bf16[1,2,32,512]{3,2,1,0:T(8,128)(2,1)S(1)}, u32[]{:S(2)}, u32[]{:S(2)}) collective-permute-start(bf16[1,2,32,512]{3,2,1,0:T(8,128)(2,1)S(1)} %pad_maximum_fusion.13), channel_id=1, source_target_pairs={{0,8},{8,16},{16,24},{1,9},{9,17},{17,25},{2,10},{10,18},{18,26},{... | collective-permute-start | bytes 196616 | tf_op jit(solution)/shard_map/ppermute | solution.py:21
  602.8 42.4 %copy-start.3 = (f32[1,2,32,256]{3,2,1,0:T(8,128)}, f32[1,2,32,256]{3,2,1,0:T(8,128)S(1)}, u32[]{:S(2)}) copy-start(f32[1,2,32,256]{3,2,1,0:T(8,128)S(1)} %get-tuple-element.37) | copy-start | bytes 196612
  606.6 26.7 %collective-permute-start.5 = (bf16[1,2,32,1024]{3,2,1,0:T(8,128)(2,1)S(1)}, bf16[1,2,32,1024]{3,2,1,0:T(8,128)(2,1)S(1)}, u32[]{:S(2)}, u32[]{:S(2)}) collective-permute-start(bf16[1,2,32,1024]{3,2,1,0:T(8,128)(2,1)S(1)} %fusion.25), channel_id=1, source_target_pairs={{8,0},{16,8},{24,16},{9,1},{17,9},{25,17},{10,2},{18,10},{26,18},{... | collective-permute-start | bytes 393224 | tf_op jit(solution)/shard_map/ppermute | solution.py:23
  607.9 25.4 %collective-permute-start.4 = (bf16[1,2,32,1024]{3,2,1,0:T(8,128)(2,1)S(1)}, bf16[1,2,32,1024]{3,2,1,0:T(8,128)(2,1)S(1)}, u32[]{:S(2)}, u32[]{:S(2)}) collective-permute-start(bf16[1,2,32,1024]{3,2,1,0:T(8,128)(2,1)S(1)} %fusion.25), channel_id=1, source_target_pairs={{0,8},{8,16},{16,24},{1,9},{9,17},{17,25},{2,10},{10,18},{18,26},{... | collective-permute-start | bytes 393224 | tf_op jit(solution)/shard_map/ppermute | solution.py:21
  634.4 10.9 copy-start.16
  634.4 11.6 copy-start.6
  682.6 980.8 %all-gather.7.cloned.1.call-start = ((), (), s32[]{:S(2)}) async-start(), calls=%async_computation.3 | async-start | bytes 32768000 | tf_op jit(solution)/shard_map/all_gather | solution.py:222
  1500.7 9.9 copy-start.17
  1500.7 9.9 copy-start.18
  1502.7 7.9 collective-permute-start.7
  1504.0 6.6 collective-permute-start.6
  1511.6 16.9 copy-start.10
  1709.0 17.4 copy-start.8
  1709.0 17.4 copy-start.13
  1709.0 17.4 copy-start.14
  1709.0 18.0 %copy-start.12 = (f32[3,256]{1,0:T(4,128)S(1)}, f32[3,256]{1,0:T(4,128)}, u32[]{:S(2)}) copy-start(f32[3,256]{1,0:T(4,128)} %param.30) | copy-start | bytes 9220
  1709.1 18.0 %copy-start.19 = (f32[3,256]{1,0:T(4,128)S(1)}, f32[3,256]{1,0:T(4,128)}, u32[]{:S(2)}) copy-start(f32[3,256]{1,0:T(4,128)} %param.32) | copy-start | bytes 9220
  1709.1 18.0 %copy-start.20 = (f32[3,256]{1,0:T(4,128)S(1)}, f32[3,256]{1,0:T(4,128)}, u32[]{:S(2)}) copy-start(f32[3,256]{1,0:T(4,128)} %param.31) | copy-start | bytes 9220
  (10 other events, 21.0 us)
Sparse Core Ops, SparseCore 0:
  12.5 504.1 all-gather.4
  682.7 817.8 reduce-scatter.1
  1502.2 161.1 all-gather.6
